TPU v7x, 32 devices: a whole 2x2x4 slice. The times are simulated.
32 devices in a mesh: occ: 8 (over z, x), aux: 4 (over y, core).
Axes of the slice: x: 2, y: 2, z: 4, core: 2. Of those that a mesh axis runs over, the one named last changes fastest.
Arguments:
- int_tiles: bfloat16 [32, 64, 128, 256], P('occ', 'aux'), may hold values from -0.5 to 0.5
- tile_ids: int32 [32, 64], P('occ', 'aux'), may hold values from 0 to 79, as said below
- tile_counts: int32 [32, 4], P('occ', 'aux'), may hold values from 8 to 16, as said below
- pair_list: int32 [64, 2], P('occ'), may hold values from 0 to 3
- occ_energy: float32 [32], replicated, may hold values from -2 to -0.5
- vir_energy: float32 [256], replicated, may hold values from 0.2 to 3
Outputs:
- gamma_tiles: bfloat16 [32, 64, 128, 256], P('occ', 'aux')
- density: float32 [256, 256], P('aux')
Inputs may be any that keep to these rules, and one draw needn't show every extreme that they name: `tile_ids`: within one orbital and one aux index's share the 16 tile numbers are distinct. Only the first tile_counts slots of a share are live; tiles and numbers of the others are never read. `pair_list`: column 0 indexes the asking occ index's orbitals, column 1 those of occ index r.
All inputs are finite; a program needn't handle non-finite values.
Results may differ from a plain program's by a relative error of at most 0.0085.
Values may be sent and summed in bfloat16 or wider, within the bound.
A program may use at most 256 MiB of HBM per device.

v0:
```python
import jax
import jax.numpy as jnp
from jax import lax
from jax.sharding import PartitionSpec as P


def amplitudes(coulomb, energy_pair, vir_energy):
    denominator = energy_pair[:, None, None] - vir_energy[None, :, None] - vir_energy[None, None, :]
    amplitude = coulomb / denominator
    return (amplitude, 2.0 * amplitude - jnp.swapaxes(amplitude, 1, 2))


def density_terms(amplitude_left, amplitude_right, spin_mixed):
    first_term = jnp.einsum(
        "rac,rbc->ab", amplitude_left, spin_mixed, precision=lax.Precision.HIGHEST
    )
    second_term = jnp.einsum(
        "rca,rcb->ab", amplitude_right, spin_mixed, precision=lax.Precision.HIGHEST
    )
    return first_term + second_term


def per_device(int_tiles, tile_ids, tile_counts, pair_list, occ_energy, vir_energy):
    peer_count = lax.axis_size("occ")
    group_count = lax.axis_size("aux")
    orb_count = int_tiles.shape[0]
    slot_count = int_tiles.shape[1]
    tile_rows = int_tiles.shape[2]
    virt_width = int_tiles.shape[3]
    pair_count = pair_list.shape[0]
    per_peer = pair_count // peer_count
    block_shape = (peer_count, per_peer, slot_count, tile_rows, virt_width)
    my_first = lax.axis_index("occ") * orb_count
    counts = tile_counts[:, 0]
    source = jnp.arange(pair_count, dtype=jnp.int32) // per_peer
    wanted = pair_list[:, 1]
    asked_for = lax.all_to_all(
        wanted.reshape(peer_count, per_peer), "occ", split_axis=0, concat_axis=0, tiled=True
    ).reshape(pair_count)
    arrived = (
        lax.all_to_all(
            int_tiles[asked_for].reshape(block_shape),
            "occ",
            split_axis=0,
            concat_axis=0,
            tiled=True,
        ),
        lax.all_to_all(
            tile_ids[asked_for].reshape(peer_count, per_peer, slot_count),
            "occ",
            split_axis=0,
            concat_axis=0,
            tiled=True,
        ),
        lax.all_to_all(
            counts[asked_for].reshape(peer_count, per_peer),
            "occ",
            split_axis=0,
            concat_axis=0,
            tiled=True,
        ),
    )
    here_index = pair_list[:, 0]
    there_global = source * orb_count + wanted
    there_tiles, there_ids, there_counts = arrived
    there_tiles = there_tiles.reshape(pair_count, slot_count, tile_rows, virt_width)
    there_ids = there_ids.reshape(pair_count, slot_count)
    there_counts = there_counts.reshape(pair_count)
    energy_pair = occ_energy[my_first + here_index] + occ_energy[there_global]
    slot_range = jnp.arange(slot_count, dtype=jnp.int32)

    def intersection_of(pair_index):
        here_orb = here_index[pair_index]
        here_live = slot_range < counts[here_orb]
        there_live = slot_range < there_counts[pair_index]
        same_tile = tile_ids[here_orb][:, None] == there_ids[pair_index][None, :]
        intersection = (same_tile & here_live[:, None] & there_live[None, :]).astype(jnp.bfloat16)
        return (int_tiles[here_orb], intersection)

    def rows_of_there(intersection, pair_index):
        return jnp.einsum(
            "st,tpb->spb", intersection, there_tiles[pair_index], preferred_element_type=jnp.float32
        ).astype(jnp.bfloat16)

    def coulomb_term(running, pair_index):
        here_block, intersection = intersection_of(pair_index)
        rows_there = rows_of_there(intersection, pair_index)
        term = lax.dot_general(
            here_block.reshape(-1, virt_width),
            rows_there.reshape(-1, virt_width),
            (((0,), (0,)), ((), ())),
            preferred_element_type=jnp.float32,
        )
        return (running, term)

    pair_range = jnp.arange(pair_count, dtype=jnp.int32)
    unused, partial_terms = lax.scan(coulomb_term, 0, pair_range)
    coulomb = lax.psum(partial_terms, "aux")
    amplitude, spin_mixed = amplitudes(coulomb, energy_pair, vir_energy)
    row_block = virt_width // group_count
    row_start = lax.axis_index("aux") * row_block
    amplitude_rows = lax.dynamic_slice_in_dim(amplitude, row_start, row_block, 1)
    amplitude_cols = lax.dynamic_slice_in_dim(amplitude, row_start, row_block, 2)
    density = density_terms(amplitude_rows, amplitude_cols, spin_mixed)
    weights = spin_mixed.astype(jnp.bfloat16)
    density = lax.psum(density.astype(jnp.bfloat16), "occ").astype(jnp.float32)
    part_shape = (slot_count, tile_rows, virt_width)

    def gamma_term(running, pair_index):
        here_block, intersection = intersection_of(pair_index)
        rows_there = rows_of_there(intersection, pair_index)
        rows_here = jnp.einsum(
            "st,spa->tpa", intersection, here_block, preferred_element_type=jnp.float32
        ).astype(jnp.bfloat16)
        pair_weights = weights[pair_index]
        here_part = lax.dot_general(
            rows_there.reshape(-1, virt_width),
            pair_weights,
            (((1,), (1,)), ((), ())),
            preferred_element_type=jnp.float32,
        )
        there_part = jnp.dot(
            rows_here.reshape(-1, virt_width), pair_weights, preferred_element_type=jnp.float32
        )
        return (
            running,
            (
                here_part.astype(jnp.bfloat16).reshape(part_shape),
                there_part.astype(jnp.bfloat16).reshape(part_shape),
            ),
        )

    unused, parts = lax.scan(gamma_term, 0, pair_range)
    here_parts, there_parts = parts
    returned = lax.all_to_all(
        there_parts.reshape(block_shape), "occ", split_axis=0, concat_axis=0, tiled=True
    ).reshape(pair_count, slot_count, tile_rows, virt_width)
    gamma_sum = jnp.zeros((orb_count, slot_count, tile_rows, virt_width), jnp.float32)
    gamma_sum = gamma_sum.at[here_index].add(here_parts.astype(jnp.float32))
    gamma_sum = gamma_sum.at[asked_for].add(returned.astype(jnp.float32))
    return (gamma_sum.astype(jnp.bfloat16), density)


def solution(mesh):
    placed = (
        P("occ", "aux", None, None),
        P("occ", "aux"),
        P("occ", "aux"),
        P("occ", None),
        P(),
        P(),
    )
    return jax.shard_map(
        per_device,
        mesh=mesh,
        in_specs=placed,
        out_specs=(P("occ", "aux", None, None), P("aux", None)),
        check_vma=False,
    )
```

profile of v0, /device:TPU:0, one launch (start us, length us, event | category | flops | bytes accessed | tf_op | source)
XLA Modules:
  0.0 811.5 jit_solution(979739568386542824)
XLA Ops:
  8.0 13.5 %all_to_all.36 = s32[8,1,1]{2,1,0:T(1,128)S(1)} all-to-all(s32[8,1,1]{2,1,0:T(1,128)S(1)} %copy.47), channel_id=1, replica_groups=mesh['occ'=8,'aux'=4] {'occ'}, dimensions={0} | all-to-all | bytes 64 | tf_op jit(solution)/shard_map/all_to_all | solution.py:37
  23.8 3.3 all-to-all-start.2
  27.1 6.9 gather_fusion.2
  34.0 6.0 all-to-all-start.3
  41.1 180.3 %all-to-all-done.3 = bf16[8,1,16,128,256]{4,3,2,1,0:T(8,128)(2,1)} async-done(((bf16[8,1,16,128,256]{4,3,2,1,0:T(8,128)(2,1)}), bf16[8,1,16,128,256]{4,3,2,1,0:T(8,128)(2,1)}, u32[]{:S(2)}, u32[]{:S(2)}) %all-to-all-start.3) | async-done | bytes 8388640 | tf_op jit(solution)/shard_map/all_to_all | solution.py:41
  221.4 3.6 all-to-all-start.1
  225.4 11.8 %copy.53 = bf16[8,16,128,256]{3,1,2,0:T(8,128)(2,1)} copy(bf16[8,16,128,256]{3,2,1,0:T(8,128)(2,1)} %bitcast.11) | data formatting | bytes 16777216
  237.2 96.8 %while.26 = (s32[]{:T(128)}, f32[8,256,256]{2,1,0:T(8,128)}, s32[8]{0:T(128)S(1)}, s32[8]{0:T(128)S(1)}, bf16[4,16,128,256]{3,2,1,0:T(8,128)(2,1)}, /*index=5*/s...) while((s32[]{:T(128)}, f32[8,256,256]{2,1,0:T(8,128)}, ...), condition=%wide.region_1.2_spmd.clone.clone, body=%wide.region_0.1_spmd.clone.clone.sunk | while | flops 285737760 | bytes 8651985 | solution.py:97
  244.8 1.7 convolution_convert_fusion.10
  269.0 1.7 convolution_convert_fusion.10
  335.5 51.5 %all-reduce.2.cloned.1.call-done = f32[8,256,256]{2,1,0:T(8,128)} async-done(((f32[8,256,256]{2,1,0:T(8,128)}), f32[8,256,256]{2,1,0:T(8,128)}) %all-reduce.2.cloned.1.call-update) | async-done | bytes 2097168 | tf_op jit(solution)/shard_map/psum | solution.py:98
  387.0 1.9 subtract_divide_fusion
  388.9 1.8 copy.52
  390.7 2.7 fusion.49
  393.4 115.8 %while.27 = (s32[]{:T(128)}, bf16[8,16,128,256]{3,2,1,0:T(8,128)(2,1)}, bf16[8,16,128,256]{3,2,1,0:T(8,128)(2,1)}, s32[8]{0:T(128)S(1)}, s32[8]{0:T(128)S(1)}, /...) while((s32[]{:T(128)}, ...), condition=%wide.region_4.5_spmd.clone.clone, body=%wide.region_3.4_spmd.clone.clone.sunk | while | flops 572524032 | bytes 19137928 | solution.py:133
  403.8 1.8 convolution_convert_fusion.13
  418.4 1.8 convolution_convert_fusion.13
  432.9 1.8 convolution_convert_fusion.13
  447.3 1.8 convolution_convert_fusion.13
  461.8 1.8 convolution_convert_fusion.13
  476.3 1.8 convolution_convert_fusion.13
  490.7 1.8 convolution_convert_fusion.13
  505.2 1.8 convolution_convert_fusion.13
  509.2 5.5 all-to-all-start.4
  514.8 11.6 %convert_element_type.39 = f32[8,16,128,256]{3,2,1,0:T(8,128)} convert(bf16[8,16,128,256]{3,2,1,0:T(8,128)(2,1)} %get-tuple-element.134) | non-fusion elementwise | flops 4194304 | bytes 25165824 | tf_op jit(solution)/shard_map/convert_element_type | solution.py:139
  527.7 2.5 fusion.40
  530.2 190.8 %psum.15 = bf16[64,256]{1,0:T(8,128)(2,1)S(1)} all-reduce(bf16[64,256]{1,0:T(8,128)(2,1)S(1)} %fusion.40), channel_id=1, replica_groups=mesh['occ'=8,'aux'=4] {'occ'}, use_global_device_ids=true, to_apply=%region_7.8 | all-reduce | flops 16384 | bytes 65536 | tf_op jit(solution)/shard_map/psum | solution.py:106
  721.6 4.3 broadcast_in_dim.16
  725.9 30.6 %scatter_fusion = f32[4,16,128,256]{3,2,1,0:T(8,128)} fusion(f32[4,16,128,256]{3,2,1,0:T(8,128)} %broadcast_in_dim.16, s32[8]{0:T(128)S(1)} %get-tuple-element.370, f32[8,16,128,256]{3,2,1,0:T(8,128)} %convert_element_type.39), kind=kCustom, calls=%fused_computation.5 | custom fusion | flops 4194304 | bytes 50331680 | tf_op jit(solution)/shard_map/scatter-add | solution.py:139
  756.5 11.5 %bitcast_convert_fusion = f32[8,16,128,256]{3,2,1,0:T(8,128)} fusion(bf16[8,1,16,128,256]{4,3,2,1,0:T(8,128)(2,1)} %all-to-all-done.4), kind=kLoop, calls=%fused_computation.64 | loop fusion | flops 4194304 | bytes 25165824 | tf_op jit(solution)/shard_map/convert_element_type | solution.py:140
  768.0 30.6 %scatter_fusion.1 = f32[4,16,128,256]{3,2,1,0:T(8,128)} fusion(f32[4,16,128,256]{3,2,1,0:T(8,128)} %scatter_fusion, s32[8]{0:T(128)S(1)} %fusion.44, f32[8,16,128,256]{3,2,1,0:T(8,128)} %bitcast_convert_fusion), kind=kCustom, calls=%fused_computation.6 | custom fusion | flops 4194304 | bytes 50331680 | tf_op jit(solution)/shard_map/scatter-add | solution.py:140
  798.6 6.0 convert_element_type.42
  (236 shorter events, 140.5 us)
Async XLA Ops:
  7.2 326.9 %copy-start = (f32[32]{0:T(128)S(1)}, f32[32]{0:T(128)}, u32[]{:S(2)}) copy-start(f32[32]{0:T(128)} %param.14) | copy-start | bytes 388
  23.8 10.2 %all-to-all-start.2 = ((s32[8,1,1]{2,1,0:T(1,128)}), s32[8,1,1]{2,1,0:T(1,128)S(1)}, u32[]{:S(2)}, u32[]{:S(2)}) async-start(s32[8,1,1]{2,1,0:T(1,128)} %copy.49), calls=%async_computation.2 | async-start | bytes 8192 | tf_op jit(solution)/shard_map/all_to_all | solution.py:55
  34.0 6.0 copy-start.4
  34.0 187.5 %all-to-all-start.3 = ((bf16[8,1,16,128,256]{4,3,2,1,0:T(8,128)(2,1)}), bf16[8,1,16,128,256]{4,3,2,1,0:T(8,128)(2,1)}, u32[]{:S(2)}, u32[]{:S(2)}) async-start(bf16[8,1,16,128,256]{4,3,2,1,0:T(8,128)(2,1)} %bitcast.165), calls=%async_computation.3 | async-start | bytes 16777216 | tf_op jit(solution)/shard_map/all_to_all | solution.py:41
  221.4 15.7 %all-to-all-start.1 = ((s32[8,1,16]{2,1,0:T(1,128)}), s32[8,1,16]{2,1,0:T(1,128)S(1)}, u32[]{:S(2)}, u32[]{:S(2)}) async-start(s32[8,1,16]{2,1,0:T(1,128)} %bitcast.5), calls=%async_computation.1 | async-start | bytes 8192 | tf_op jit(solution)/shard_map/all_to_all | solution.py:48
  225.1 161.9 %all-reduce.2.cloned.1.call-start = ((), (), s32[]{:S(2)}) async-start(), calls=%async_computation.5 | async-start | bytes 4194304 | tf_op jit(solution)/shard_map/psum | solution.py:98
  225.3 11.8 %copy-start.2 = (s32[4,1]{0,1:T(1,128)S(1)}, s32[4,1]{0,1:T(1,128)}, u32[]{:S(2)}) copy-start(s32[4,1]{0,1:T(1,128)} %param.12) | copy-start | bytes 52
  237.2 98.2 %copy-start.5 = (f32[256]{0:T(256)S(1)}, f32[256]{0:T(256)}, u32[]{:S(2)}) copy-start(f32[256]{0:T(256)} %param.15) | copy-start | bytes 3076
  509.2 247.3 %all-to-all-start.4 = ((bf16[8,1,16,128,256]{4,3,2,1,0:T(8,128)(2,1)}), bf16[8,1,16,128,256]{4,3,2,1,0:T(8,128)(2,1)}, u32[]{:S(2)}, u32[]{:S(2)}) async-start(bf16[8,1,16,128,256]{4,3,2,1,0:T(8,128)(2,1)} %bitcast.166), calls=%async_computation.4 | async-start | bytes 16777216 | tf_op jit(solution)/shard_map/all_to_all | solution.py:135
  514.8 11.6 %copy-start.3 = (f32[8,256,256]{1,2,0:T(8,128)S(1)}, f32[8,256,256]{1,2,0:T(8,128)}, u32[]{:S(2)}) copy-start(f32[8,256,256]{1,2,0:T(8,128)} %copy.52) | copy-start | bytes 6291460
  768.0 36.6 %copy-start.1 = (f32[32]{0:T(128)S(1)}, f32[32]{0:T(128)}, u32[]{:S(2)}) copy-start(f32[32]{0:T(128)} %param.14) | copy-start | bytes 388
Sparse Core Ops, SparseCore 0:
  334.2 52.7 all-reduce.1
where the time goes:
time: 815 us; the launch traced here: 811 us
  waiting for transfers between devices  232 us (28%)
  blocking collectives  204 us (25%)
  other arithmetic  117 us (14%)
  local copies, waits for them, and re-layouts  109 us (13%)
  loops' own time  62.4 us (8%)
  matrix products  54.3 us (7%)
  starting transfers between devices  18.5 us (2%)
  between operations  14.2 us (2%)
    psum x1, blocking collectives, per_device(): density = lax.psum(density.astype(jnp.bfloat16), 'occ').astype(jnp.float32)  191 us
    all_to_all x1, waiting for transfers between devices, per_device(): lax.all_to_all(int_tiles[asked_for].reshape(block_shape), 'occ', split_ax...  180 us
    psum x1, waiting for transfers between devices, per_device(): coulomb = lax.psum(partial_terms, 'aux')  51.5 us
    another operation x1, loops' own time, per_device(): unused, partial_terms = lax.scan(coulomb_term, 0, pair_range)  31.4 us
    another operation x1, loops' own time, per_device(): unused, parts = lax.scan(gamma_term, 0, pair_range)  31 us
    scatter-add x1, other arithmetic, per_device(): gamma_sum = gamma_sum.at[here_index].add(here_parts.astype(jnp.float32))  30.6 us
    scatter-add x1, other arithmetic, per_device(): gamma_sum = gamma_sum.at[asked_for].add(returned.astype(jnp.float32))  30.6 us
    dot_general x16, matrix products, rows_of_there(): jnp.einsum('st,tpb->spb', intersection, there_tiles[pair_index], preferre...  27.9 us
  transfers between devices with their start and end apart: 5, of which 2 were waited for; matrix products, arithmetic and copies ran while one was open for 9% of the time, Pallas kernels for 0%

commit v1 on v0

--- a/solution.py
+++ b/solution.py
@@ -2,6 +2,29 @@
 import jax.numpy as jnp
 from jax import lax
 from jax.sharding import PartitionSpec as P
+
+
+def cut_along(x, dim, size):
+    shape = x.shape
+    blocks = x.reshape(*shape[:dim], size, shape[dim] // size, *shape[dim + 1 :])
+    return jnp.moveaxis(blocks, dim, 0)
+
+
+def in_order(blocks, dim):
+    shape = list(blocks.shape[1:])
+    shape[dim] *= blocks.shape[0]
+    return jnp.moveaxis(blocks, 0, dim).reshape(shape)
+
+
+def pairwise_exchange(array, axis, split_dim, concat_dim):
+    size, index = (lax.axis_size(axis), lax.axis_index(axis))
+    pieces = cut_along(array, split_dim, size)
+    finished = [pieces[index]]
+    for lap in range(1, size):
+        sent = pieces[index ^ lap]
+        finished.append(lax.ppermute(sent, axis, [(i, i ^ lap) for i in range(size)]))
+    pieces = jnp.stack(finished)[index ^ jnp.arange(size)]
+    return in_order(pieces, concat_dim)
 
 
 def amplitudes(coulomb, energy_pair, vir_energy):
@@ -38,13 +61,7 @@
         wanted.reshape(peer_count, per_peer), "occ", split_axis=0, concat_axis=0, tiled=True
     ).reshape(pair_count)
     arrived = (
-        lax.all_to_all(
-            int_tiles[asked_for].reshape(block_shape),
-            "occ",
-            split_axis=0,
-            concat_axis=0,
-            tiled=True,
-        ),
+        pairwise_exchange(int_tiles[asked_for].reshape(block_shape), "occ", 0, 0),
         lax.all_to_all(
             tile_ids[asked_for].reshape(peer_count, per_peer, slot_count),
             "occ",

time: 815 us -> 830 us (1.018)
  local copies, waits for them, and re-layouts: 109 us -> 140 us
  waiting for transfers between devices: 232 us -> 207 us
  starting transfers between devices: 18.5 us -> 30.9 us
    all_to_all x1, waiting for transfers between devices: 180 us -> 6.39 us  [per_device(): lax.all_to_all(wanted.reshape(peer_count, per_peer), 'occ', split_axis=0,...]
    all_to_all x1, waiting for transfers between devices: 0.01 us -> 80.3 us  [per_device(): lax.all_to_all(counts[asked_for].reshape(peer_count, per_peer), 'occ', sp...]
    psum x1, waiting for transfers between devices: 51.5 us -> 92.3 us  [per_device(): coulomb = lax.psum(partial_terms, 'aux')]
    ppermute x0 -> x7, waiting for transfers between devices: none -> 27.5 us  [pairwise_exchange(): lax.ppermute(sent, axis, [(i, i ^ lap) for i in range(size)])]
    unnamed x13 -> x18, local copies, waits for them, and re-layouts: 11.8 us -> 26.8 us
    all_to_all x1 -> x0, blocking collectives: 13.5 us -> none  [per_device(): lax.all_to_all(wanted.reshape(peer_count, per_peer), 'occ', split_axis=0,...]
    ppermute x0 -> x7, starting transfers between devices: none -> 11.5 us  [pairwise_exchange(): lax.ppermute(sent, axis, [(i, i ^ lap) for i in range(size)])]
    psum x1, blocking collectives: 191 us -> 199 us  [per_device(): density = lax.psum(density.astype(jnp.bfloat16), 'occ').astype(jnp.float32)]
  transfers between devices with their start and end apart: 5 -> 12, of which waited for: 2 -> 5; matrix products, arithmetic and copies ran while one was open for 9% -> 11% of each run, Pallas kernels for 0% -> 0%
where the time goes in v1:
time: 830 us; the launch traced here: 827 us
  waiting for transfers between devices  207 us (25%)
  blocking collectives  199 us (24%)
  local copies, waits for them, and re-layouts  140 us (17%)
  other arithmetic  117 us (14%)
  loops' own time  61.8 us (7%)
  matrix products  57.5 us (7%)
  starting transfers between devices  30.9 us (4%)
  between operations  14.2 us (2%)
    psum x1, blocking collectives, per_device(): density = lax.psum(density.astype(jnp.bfloat16), 'occ').astype(jnp.float32)  199 us
    psum x1, waiting for transfers between devices, per_device(): coulomb = lax.psum(partial_terms, 'aux')  92.3 us
    all_to_all x1, waiting for transfers between devices, per_device(): lax.all_to_all(counts[asked_for].reshape(peer_count, per_peer), 'occ', sp...  80.3 us
    another operation x1, loops' own time, per_device(): unused, partial_terms = lax.scan(coulomb_term, 0, pair_range)  31.4 us
    scatter-add x1, other arithmetic, per_device(): gamma_sum = gamma_sum.at[here_index].add(here_parts.astype(jnp.float32))  30.6 us
    scatter-add x1, other arithmetic, per_device(): gamma_sum = gamma_sum.at[asked_for].add(returned.astype(jnp.float32))  30.6 us
    another operation x1, loops' own time, per_device(): unused, parts = lax.scan(gamma_term, 0, pair_range)  30.4 us
    dot_general x16, matrix products, rows_of_there(): jnp.einsum('st,tpb->spb', intersection, there_tiles[pair_index], preferre...  27.9 us
  transfers between devices with their start and end apart: 12, of which 5 were waited for; matrix products, arithmetic and copies ran while one was open for 11% of the time, Pallas kernels for 0%

profile of v1, /device:TPU:0, one launch (start us, length us, event | category | flops | bytes accessed | tf_op | source)
XLA Modules:
  0.0 827.0 jit_solution(12980642913439680115)
XLA Ops:
  8.6 7.3 all-to-all-start
  15.9 6.4 all-to-all-done
  22.5 6.9 gather_fusion.2
  29.4 5.6 dynamic-slice_bitcast_fusion
  36.1 2.4 collective-permute-start.2
  42.6 3.3 all-to-all-start.2
  45.9 2.4 bitcast_dynamic-update-slice_fusion.7
  49.5 80.3 %all-to-all-done.2 = s32[8,1,1]{2,1,0:T(1,128)S(1)} async-done(((s32[8,1,1]{2,1,0:T(1,128)}), s32[8,1,1]{2,1,0:T(1,128)S(1)}, u32[]{:S(2)}, u32[]{:S(2)}) %all-to-all-start.2) | async-done | bytes 64 | tf_op jit(solution)/shard_map/all_to_all | solution.py:72
  129.8 3.3 all-to-all-start.1
  133.4 3.8 collective-permute-start.5
  140.8 2.3 bitcast_dynamic-update-slice_fusion.5
  143.2 2.3 bitcast_dynamic-update-slice_fusion.4
  145.5 2.4 bitcast_dynamic-update-slice_fusion.3
  147.9 2.3 bitcast_dynamic-update-slice_fusion.2
  150.2 11.2 %collective-permute-done.5 = bf16[1,1,16,128,256]{4,3,2,1,0:T(8,128)(2,1)S(1)} collective-permute-done((bf16[1,1,16,128,256]{4,3,2,1,0:T(8,128)(2,1)S(1)}, bf16[1,1,16,128,256]{4,3,2,1,0:T(8,128)(2,1)S(1)}, u32[]{:S(2)}, u32[]{:S(2)}) %collective-permute-start.5) | collective-permute-done | bytes 1048608 | tf_op jit(solution)/shard_map/ppermute | solution.py:25
  162.4 16.3 %collective-permute-done.6 = bf16[1,1,16,128,256]{4,3,2,1,0:T(8,128)(2,1)S(1)} collective-permute-done((bf16[1,1,16,128,256]{4,3,2,1,0:T(8,128)(2,1)S(1)}, bf16[1,1,16,128,256]{4,3,2,1,0:T(8,128)(2,1)S(1)}, u32[]{:S(2)}, u32[]{:S(2)}) %collective-permute-start.6) | collective-permute-done | bytes 1048608 | tf_op jit(solution)/shard_map/ppermute | solution.py:25
  179.8 8.2 gather_fusion.3
  188.0 11.8 %copy.51 = bf16[8,16,128,256]{3,1,2,0:T(8,128)(2,1)} copy(bf16[8,16,128,256]{3,2,1,0:T(8,128)(2,1)} %gather_fusion.3) | data formatting | bytes 16777216
  199.8 97.0 %while.26 = (s32[]{:T(128)}, f32[8,256,256]{2,1,0:T(8,128)}, s32[8]{0:T(128)S(1)}, s32[8]{0:T(128)S(1)}, bf16[4,16,128,256]{3,2,1,0:T(8,128)(2,1)}, /*index=5*/s...) while((s32[]{:T(128)}, f32[8,256,256]{2,1,0:T(8,128)}, ...), condition=%wide.region_1.2_spmd.clone.clone, body=%wide.region_0.1_spmd.clone.clone.sunk | while | flops 285737760 | bytes 8651985 | solution.py:114
  298.3 92.3 %all-reduce.2.cloned.1.call-done = f32[8,256,256]{2,1,0:T(8,128)} async-done(((f32[8,256,256]{2,1,0:T(8,128)}), f32[8,256,256]{2,1,0:T(8,128)}) %all-reduce.2.cloned.1.call-update) | async-done | bytes 2097168 | tf_op jit(solution)/shard_map/psum | solution.py:115
  394.4 2.7 fusion.50
  397.0 116.3 %while.27 = (s32[]{:T(128)}, bf16[8,16,128,256]{3,2,1,0:T(8,128)(2,1)}, bf16[8,16,128,256]{3,2,1,0:T(8,128)(2,1)}, s32[8]{0:T(128)S(1)}, s32[8]{0:T(128)S(1)}, /...) while((s32[]{:T(128)}, ...), condition=%wide.region_4.5_spmd.clone.clone, body=%wide.region_3.4_spmd.clone.clone.sunk | while | flops 572524032 | bytes 19137928 | solution.py:150
  513.3 5.5 all-to-all-start.3
  518.8 2.9 convolution_bitcast_fusion.2
  521.7 4.1 fusion.40
  525.8 199.3 %psum.15 = bf16[64,256]{1,0:T(8,128)(2,1)S(1)} all-reduce(bf16[64,256]{1,0:T(8,128)(2,1)S(1)} %fusion.40), channel_id=1, replica_groups=mesh['occ'=8,'aux'=4] {'occ'}, use_global_device_ids=true, to_apply=%region_7.8 | all-reduce | flops 16384 | bytes 65536 | tf_op jit(solution)/shard_map/psum | solution.py:123
  725.7 11.5 %convert_element_type.39 = f32[8,16,128,256]{3,2,1,0:T(8,128)} convert(bf16[8,16,128,256]{3,2,1,0:T(8,128)(2,1)} %get-tuple-element.134) | non-fusion elementwise | flops 4194304 | bytes 25165824 | tf_op jit(solution)/shard_map/convert_element_type | solution.py:156
  737.2 4.3 broadcast_in_dim.16
  741.5 30.6 %scatter_fusion = f32[4,16,128,256]{3,2,1,0:T(8,128)} fusion(f32[4,16,128,256]{3,2,1,0:T(8,128)} %broadcast_in_dim.16, s32[8]{0:T(128)S(1)} %get-tuple-element.377, f32[8,16,128,256]{3,2,1,0:T(8,128)} %convert_element_type.39), kind=kCustom, calls=%fused_computation.6 | custom fusion | flops 4194304 | bytes 50331680 | tf_op jit(solution)/shard_map/scatter-add | solution.py:156
  772.1 11.5 %bitcast_convert_fusion = f32[8,16,128,256]{3,2,1,0:T(8,128)} fusion(bf16[8,1,16,128,256]{4,3,2,1,0:T(8,128)(2,1)} %all-to-all-done.3), kind=kLoop, calls=%fused_computation.65 | loop fusion | flops 4194304 | bytes 25165824 | tf_op jit(solution)/shard_map/convert_element_type | solution.py:157
  783.6 30.6 %scatter_fusion.1 = f32[4,16,128,256]{3,2,1,0:T(8,128)} fusion(f32[4,16,128,256]{3,2,1,0:T(8,128)} %scatter_fusion, s32[8]{0:T(128)S(1)} %fusion.46, f32[8,16,128,256]{3,2,1,0:T(8,128)} %bitcast_convert_fusion), kind=kCustom, calls=%fused_computation.7 | custom fusion | flops 4194304 | bytes 50331680 | tf_op jit(solution)/shard_map/scatter-add | solution.py:157
  814.1 6.0 convert_element_type.42
  (259 shorter events, 171.5 us)
Async XLA Ops:
  7.2 289.8 %copy-start = (f32[32]{0:T(128)S(1)}, f32[32]{0:T(128)}, u32[]{:S(2)}) copy-start(f32[32]{0:T(128)} %param.14) | copy-start | bytes 388
  8.6 13.6 %all-to-all-start = ((s32[8,1,1]{2,1,0:T(1,128)}), s32[8,1,1]{2,1,0:T(1,128)S(1)}, u32[]{:S(2)}, u32[]{:S(2)}) async-start(s32[8,1,1]{2,1,0:T(1,128)} %copy.46), calls=%async_computation | async-start | bytes 8192 | tf_op jit(solution)/shard_map/all_to_all | solution.py:60
  29.4 11.9 %copy-start.2 = (s32[4,1]{0,1:T(1,128)S(1)}, s32[4,1]{0,1:T(1,128)}, u32[]{:S(2)}) copy-start(s32[4,1]{0,1:T(1,128)} %param.12) | copy-start | bytes 52
  29.4 18.9 %copy-start.3 = (s32[4,16]{1,0:T(4,128)S(1)}, s32[4,16]{1,0:T(4,128)}, u32[]{:S(2)}) copy-start(s32[4,16]{1,0:T(4,128)} %param.11) | copy-start | bytes 772
  35.0 98.4 %collective-permute-start = (bf16[1,1,16,128,256]{4,3,2,1,0:T(8,128)(2,1)}, bf16[1,1,16,128,256]{4,3,2,1,0:T(8,128)(2,1)}, u32[]{:S(2)}, u32[]{:S(2)}) collective-permute-start(bf16[1,1,16,128,256]{4,3,2,1,0:T(8,128)(2,1)} %get-tuple-element.374), channel_id=1, source_target_pairs={{0,4},{4,0},{8,12},{12,8},{16,20},{20,16},{24,28},{28,24},{1,5},{5... | collective-permute-start | bytes 3145736 | tf_op jit(solution)/shard_map/ppermute | solution.py:25
  35.4 104.0 %collective-permute-start.1 = (bf16[1,1,16,128,256]{4,3,2,1,0:T(8,128)(2,1)}, bf16[1,1,16,128,256]{4,3,2,1,0:T(8,128)(2,1)}, u32[]{:S(2)}, u32[]{:S(2)}) collective-permute-start(bf16[1,1,16,128,256]{4,3,2,1,0:T(8,128)(2,1)} %get-tuple-element.373), channel_id=1, source_target_pairs={{0,8},{4,12},{8,0},{12,4},{16,24},{20,28},{24,16},{28,20},{1,9},{5... | collective-permute-start | bytes 3145736 | tf_op jit(solution)/shard_map/ppermute | solution.py:25
  36.1 107.1 %collective-permute-start.2 = (bf16[1,1,16,128,256]{4,3,2,1,0:T(8,128)(2,1)}, bf16[1,1,16,128,256]{4,3,2,1,0:T(8,128)(2,1)}, u32[]{:S(2)}, u32[]{:S(2)}) collective-permute-start(bf16[1,1,16,128,256]{4,3,2,1,0:T(8,128)(2,1)} %get-tuple-element.372), channel_id=1, source_target_pairs={{0,12},{4,8},{8,4},{12,0},{16,28},{20,24},{24,20},{28,16},{1,13},{... | collective-permute-start | bytes 3145736 | tf_op jit(solution)/shard_map/ppermute | solution.py:25
  38.5 107.0 %collective-permute-start.3 = (bf16[1,1,16,128,256]{4,3,2,1,0:T(8,128)(2,1)}, bf16[1,1,16,128,256]{4,3,2,1,0:T(8,128)(2,1)}, u32[]{:S(2)}, u32[]{:S(2)}) collective-permute-start(bf16[1,1,16,128,256]{4,3,2,1,0:T(8,128)(2,1)} %get-tuple-element.371), channel_id=1, source_target_pairs={{0,16},{4,20},{8,24},{12,28},{16,0},{20,4},{24,8},{28,12},{1,17},{... | collective-permute-start | bytes 3145736 | tf_op jit(solution)/shard_map/ppermute | solution.py:25
  39.0 108.8 %collective-permute-start.4 = (bf16[1,1,16,128,256]{4,3,2,1,0:T(8,128)(2,1)S(1)}, bf16[1,1,16,128,256]{4,3,2,1,0:T(8,128)(2,1)}, u32[]{:S(2)}, u32[]{:S(2)}) collective-permute-start(bf16[1,1,16,128,256]{4,3,2,1,0:T(8,128)(2,1)S(1)} %get-tuple-element.370), channel_id=1, source_target_pairs={{0,20},{4,16},{8,28},{12,24},{16,4},{20,0},{24,12},{28,8},{1,21},{... | collective-permute-start | bytes 3145736 | tf_op jit(solution)/shard_map/ppermute | solution.py:25
  42.6 87.1 %all-to-all-start.2 = ((s32[8,1,1]{2,1,0:T(1,128)}), s32[8,1,1]{2,1,0:T(1,128)S(1)}, u32[]{:S(2)}, u32[]{:S(2)}) async-start(s32[8,1,1]{2,1,0:T(1,128)} %copy.48), calls=%async_computation.2 | async-start | bytes 8192 | tf_op jit(solution)/shard_map/all_to_all | solution.py:72
  129.8 70.1 %all-to-all-start.1 = ((s32[8,1,16]{2,1,0:T(1,128)}), s32[8,1,16]{2,1,0:T(1,128)S(1)}, u32[]{:S(2)}, u32[]{:S(2)}) async-start(s32[8,1,16]{2,1,0:T(1,128)} %bitcast.5), calls=%async_computation.1 | async-start | bytes 8192 | tf_op jit(solution)/shard_map/all_to_all | solution.py:65
  133.1 257.5 %all-reduce.2.cloned.1.call-start = ((), (), s32[]{:S(2)}) async-start(), calls=%async_computation.4 | async-start | bytes 4194304 | tf_op jit(solution)/shard_map/psum | solution.py:115
  133.4 28.0 %collective-permute-start.5 = (bf16[1,1,16,128,256]{4,3,2,1,0:T(8,128)(2,1)S(1)}, bf16[1,1,16,128,256]{4,3,2,1,0:T(8,128)(2,1)S(1)}, u32[]{:S(2)}, u32[]{:S(2)}) collective-permute-start(bf16[1,1,16,128,256]{4,3,2,1,0:T(8,128)(2,1)S(1)} %get-tuple-element.369), channel_id=1, source_target_pairs={{0,24},{4,28},{8,16},{12,20},{16,8},{20,12},{24,0},{28,4},{1,25},{... | collective-permute-start | bytes 3145736 | tf_op jit(solution)/shard_map/ppermute | solution.py:25
  139.4 39.3 %collective-permute-start.6 = (bf16[1,1,16,128,256]{4,3,2,1,0:T(8,128)(2,1)S(1)}, bf16[1,1,16,128,256]{4,3,2,1,0:T(8,128)(2,1)S(1)}, u32[]{:S(2)}, u32[]{:S(2)}) collective-permute-start(bf16[1,1,16,128,256]{4,3,2,1,0:T(8,128)(2,1)S(1)} %get-tuple-element.368), channel_id=1, source_target_pairs={{0,28},{4,24},{8,20},{12,16},{16,12},{20,8},{24,4},{28,0},{1,29},{... | collective-permute-start | bytes 3145736 | tf_op jit(solution)/shard_map/ppermute | solution.py:25
  199.8 98.4 %copy-start.4 = (f32[256]{0:T(256)S(1)}, f32[256]{0:T(256)}, u32[]{:S(2)}) copy-start(f32[256]{0:T(256)} %param.15) | copy-start | bytes 3076
  513.3 258.8 %all-to-all-start.3 = ((bf16[8,1,16,128,256]{4,3,2,1,0:T(8,128)(2,1)}), bf16[8,1,16,128,256]{4,3,2,1,0:T(8,128)(2,1)}, u32[]{:S(2)}, u32[]{:S(2)}) async-start(bf16[8,1,16,128,256]{4,3,2,1,0:T(8,128)(2,1)} %bitcast.195), calls=%async_computation.3 | async-start | bytes 16777216 | tf_op jit(solution)/shard_map/all_to_all | solution.py:152
  783.6 36.6 %copy-start.1 = (f32[32]{0:T(128)S(1)}, f32[32]{0:T(128)}, u32[]{:S(2)}) copy-start(f32[32]{0:T(128)} %param.14) | copy-start | bytes 388
Sparse Core Ops, SparseCore 0:
  297.0 93.5 all-reduce.1
